TPU v7x, 256 devices: a whole 4x4x8 slice. The times are simulated.
256 devices in a mesh: row: 32 (over x_hi, z, core), col: 8 (over y, x_lo).
Axes of the slice: x: 4 (x_hi: 2, x_lo: 2; x = x_hi * 2 + x_lo), y: 4, z: 8, core: 2. Of those that a mesh axis runs over, the one named last changes fastest.
Arguments:
- p_tiles: bfloat16 [1024, 2, 128, 128], P(('row', 'col')), may hold values from -0.5 to 0.5
- p_cols: int32 [1024, 2], P(('row', 'col')), may hold values from 0 to 31, as said below
- q_tiles: bfloat16 [1024, 6, 128, 128], P(('row', 'col')), may hold values from -1.796875 to 1.796875
- q_cols: int32 [1024, 6], P(('row', 'col')), may hold values from 0 to 31, all different within a row
Outputs:
- coarse: float32 [4096, 4096], P('row', 'col')
Inputs may be any that keep to these rules, and one draw needn't show every extreme that they name: `p_cols`: the 2 coarse tiles in one row differ; among the fine blocks held by the devices of one index of col, every coarse tile is named at least once and at most 16 times, and some tile exactly 16 times. `q_cols`: the 6 coarse tiles in one row differ; every coarse tile appears somewhere.
All inputs are finite; a program needn't handle non-finite values.
Results may differ from a plain program's by a relative error of at most 0.0003.
Values may be sent and summed in bfloat16 or wider, within the bound.
A program may use at most 128 MiB of HBM per device.

v0:
```python
import math
import jax
import jax.numpy as jnp
from jax import lax
from jax.sharding import PartitionSpec as P


def spread_tiles(tile_set, columns, tile_count):
    blocks, per_block, extent, _ = tile_set.shape
    flipped = jnp.swapaxes(tile_set, 2, 3)
    fine_ids = jnp.broadcast_to(jnp.arange(blocks, dtype=jnp.int32)[:, None], (blocks, per_block))
    placed = jnp.zeros((tile_count, extent, blocks, extent), tile_set.dtype)
    placed = placed.at[columns, :, fine_ids, :].set(flipped)
    return placed.reshape(tile_count * extent, blocks * extent)


def fold_tiles(summed, transposed, tile_set, columns):
    blocks, per_block, extent, _ = tile_set.shape
    height = transposed.shape[0]
    bundle = math.gcd(blocks, 8)
    tile_groups = tile_set.reshape(blocks // bundle, bundle, per_block, extent, extent)
    column_groups = columns.reshape(blocks // bundle, bundle * per_block)

    def one_group(running, inputs):
        position, bundle_tiles, coarse_ids = inputs
        offset = position * bundle * extent
        stripe = lax.dynamic_slice_in_dim(transposed, offset, bundle * extent, 1).reshape(
            height, bundle, extent
        )
        product = jnp.einsum(
            "rfa,fkab->rfkb", stripe, bundle_tiles, preferred_element_type=jnp.float32
        )
        tiled = running.reshape(height, -1, extent)
        tiled = tiled.at[:, coarse_ids, :].add(product.reshape(height, bundle * per_block, extent))
        return (tiled.reshape(height, -1), None)

    counter = jnp.arange(blocks // bundle, dtype=jnp.int32)
    summed, _ = lax.scan(one_group, summed, (counter, tile_groups, column_groups))
    return summed


def body(p_tiles, p_cols, q_tiles, q_cols):
    extent = p_tiles.shape[2]
    tile_count = lax.axis_size("row")
    expanded = spread_tiles(p_tiles, p_cols, tile_count)
    transposed = lax.all_to_all(expanded, "row", split_axis=0, concat_axis=1, tiled=True)
    empty = jnp.zeros((transposed.shape[0], tile_count * extent), jnp.float32)
    partial_sum = fold_tiles(
        empty,
        transposed,
        lax.all_gather(q_tiles, "row", axis=0, tiled=True),
        lax.all_gather(q_cols, "row", axis=0, tiled=True),
    )
    return lax.psum_scatter(partial_sum, "col", scatter_dimension=1, tiled=True)


def solution(mesh):
    placed = (
        P(("row", "col"), None, None, None),
        P(("row", "col"), None),
        P(("row", "col"), None, None, None),
        P(("row", "col"), None),
    )
    return jax.shard_map(
        body, mesh=mesh, in_specs=placed, out_specs=P("row", "col"), check_vma=False
    )
```

profile of v0, /device:TPU:1, one launch (start us, length us, event | category | flops | bytes accessed | tf_op | source)
XLA Modules:
  0.0 604.4 jit_solution(11690526982969184347)
XLA Ops:
  9.3 3.0 broadcast_in_dim.18
  14.5 6.5 %copy.24 = bf16[32,128,4,128]{1,3,2,0:T(8,128)(2,1)} copy(bf16[32,128,4,128]{3,1,2,0:T(8,128)(2,1)} %scatter_fusion.1) | data formatting | bytes 8388608 | tf_op jit(solution)/shard_map/scatter | solution.py:13
  21.0 12.8 %all-to-all-start = ((bf16[32,128,512]{1,2,0:T(8,128)(2,1)}), bf16[32,128,512]{1,2,0:T(8,128)(2,1)}, u32[]{:S(2)}, u32[]{:S(2)}) async-start(bf16[32,128,512]{1,2,0:T(8,128)(2,1)} %bitcast.65), calls=%async_computation | async-start | bytes 8388608 | tf_op jit(solution)/shard_map/all_to_all | solution.py:46
  33.8 154.7 %all-gather = s32[32,4,6]{2,1,0:T(4,128)S(1)} all-gather(s32[1,4,6]{2,1,0:T(4,128)S(1)} %bitcast.68), channel_id=1, replica_groups=mesh['row'=32,'col'=8] {'row'}, dimensions={0}, use_global_device_ids=true | all-gather | bytes 3168 | tf_op jit(solution)/shard_map/all_gather | solution.py:52
  188.6 77.6 %all-gather.3.cloned.1.call-done = bf16[128,6,128,128]{3,2,1,0:T(8,128)(2,1)} async-done(((bf16[4,6,128,128]{3,2,1,0:T(8,128)(2,1)}), bf16[128,6,128,128]{3,2,1,0:T(8,128)(2,1)}) %all-gather.3.cloned.1.call-update) | async-done | bytes 25165840 | tf_op jit(solution)/shard_map/all_gather | solution.py:51
  267.7 274.9 %while.12 = (s32[]{:T(128)}, f32[128,4096]{0,1:T(8,128)}, s32[16,48]{1,0:T(8,128)S(1)}, bf16[16,8,6,128,128]{4,3,2,1,0:T(8,128)(2,1)}, s32[16]{0:T(128)S(1)}, /*...) while((s32[]{:T(128)}, f32[128,4096]{0,1:T(8,128)}, ...), condition=%wide.region_3.4_spmd, body=%wide.region_1.3_spmd.sunk | while | flops 202113168 | bytes 29623528 | solution.py:38
  276.3 6.7 %scatter_fusion = f32[128,32,128]{2,0,1:T(8,128)S(1)} fusion(f32[128,32,128]{2,0,1:T(8,128)S(1)} %copy.34, s32[48]{0:T(128)S(1)} %fusion.16, f32[48,128,128]{2,1,0:T(8,128)} %bitcast.61), kind=kCustom, calls=%fused_computation.clone.1 | custom fusion | flops 786432 | bytes 9437376 | tf_op jit(solution)/shard_map/while/body/eval_jaxpr/scatter-add | solution.py:34
  289.2 2.4 copy.35
  293.5 6.7 %scatter_fusion = f32[128,32,128]{2,0,1:T(8,128)S(1)} fusion(f32[128,32,128]{2,0,1:T(8,128)S(1)} %copy.34, s32[48]{0:T(128)S(1)} %fusion.16, f32[48,128,128]{2,1,0:T(8,128)} %bitcast.61), kind=kCustom, calls=%fused_computation.clone.1 | custom fusion | flops 786432 | bytes 9437376 | tf_op jit(solution)/shard_map/while/body/eval_jaxpr/scatter-add | solution.py:34
  310.7 6.7 %scatter_fusion = f32[128,32,128]{2,0,1:T(8,128)S(1)} fusion(f32[128,32,128]{2,0,1:T(8,128)S(1)} %copy.34, s32[48]{0:T(128)S(1)} %fusion.16, f32[48,128,128]{2,1,0:T(8,128)} %bitcast.61), kind=kCustom, calls=%fused_computation.clone.1 | custom fusion | flops 786432 | bytes 9437376 | tf_op jit(solution)/shard_map/while/body/eval_jaxpr/scatter-add | solution.py:34
  323.5 2.4 copy.35
  327.8 6.7 %scatter_fusion = f32[128,32,128]{2,0,1:T(8,128)S(1)} fusion(f32[128,32,128]{2,0,1:T(8,128)S(1)} %copy.34, s32[48]{0:T(128)S(1)} %fusion.16, f32[48,128,128]{2,1,0:T(8,128)} %bitcast.61), kind=kCustom, calls=%fused_computation.clone.1 | custom fusion | flops 786432 | bytes 9437376 | tf_op jit(solution)/shard_map/while/body/eval_jaxpr/scatter-add | solution.py:34
  340.7 2.4 copy.35
  345.0 6.7 %scatter_fusion = f32[128,32,128]{2,0,1:T(8,128)S(1)} fusion(f32[128,32,128]{2,0,1:T(8,128)S(1)} %copy.34, s32[48]{0:T(128)S(1)} %fusion.16, f32[48,128,128]{2,1,0:T(8,128)} %bitcast.61), kind=kCustom, calls=%fused_computation.clone.1 | custom fusion | flops 786432 | bytes 9437376 | tf_op jit(solution)/shard_map/while/body/eval_jaxpr/scatter-add | solution.py:34
  357.9 2.4 copy.35
  362.2 6.7 %scatter_fusion = f32[128,32,128]{2,0,1:T(8,128)S(1)} fusion(f32[128,32,128]{2,0,1:T(8,128)S(1)} %copy.34, s32[48]{0:T(128)S(1)} %fusion.16, f32[48,128,128]{2,1,0:T(8,128)} %bitcast.61), kind=kCustom, calls=%fused_computation.clone.1 | custom fusion | flops 786432 | bytes 9437376 | tf_op jit(solution)/shard_map/while/body/eval_jaxpr/scatter-add | solution.py:34
  375.1 2.4 copy.35
  379.4 6.7 %scatter_fusion = f32[128,32,128]{2,0,1:T(8,128)S(1)} fusion(f32[128,32,128]{2,0,1:T(8,128)S(1)} %copy.34, s32[48]{0:T(128)S(1)} %fusion.16, f32[48,128,128]{2,1,0:T(8,128)} %bitcast.61), kind=kCustom, calls=%fused_computation.clone.1 | custom fusion | flops 786432 | bytes 9437376 | tf_op jit(solution)/shard_map/while/body/eval_jaxpr/scatter-add | solution.py:34
  392.3 2.4 copy.35
  396.6 6.7 %scatter_fusion = f32[128,32,128]{2,0,1:T(8,128)S(1)} fusion(f32[128,32,128]{2,0,1:T(8,128)S(1)} %copy.34, s32[48]{0:T(128)S(1)} %fusion.16, f32[48,128,128]{2,1,0:T(8,128)} %bitcast.61), kind=kCustom, calls=%fused_computation.clone.1 | custom fusion | flops 786432 | bytes 9437376 | tf_op jit(solution)/shard_map/while/body/eval_jaxpr/scatter-add | solution.py:34
  409.4 2.4 copy.35
  413.7 6.7 %scatter_fusion = f32[128,32,128]{2,0,1:T(8,128)S(1)} fusion(f32[128,32,128]{2,0,1:T(8,128)S(1)} %copy.34, s32[48]{0:T(128)S(1)} %fusion.16, f32[48,128,128]{2,1,0:T(8,128)} %bitcast.61), kind=kCustom, calls=%fused_computation.clone.1 | custom fusion | flops 786432 | bytes 9437376 | tf_op jit(solution)/shard_map/while/body/eval_jaxpr/scatter-add | solution.py:34
  430.9 6.7 %scatter_fusion = f32[128,32,128]{2,0,1:T(8,128)S(1)} fusion(f32[128,32,128]{2,0,1:T(8,128)S(1)} %copy.34, s32[48]{0:T(128)S(1)} %fusion.16, f32[48,128,128]{2,1,0:T(8,128)} %bitcast.61), kind=kCustom, calls=%fused_computation.clone.1 | custom fusion | flops 786432 | bytes 9437376 | tf_op jit(solution)/shard_map/while/body/eval_jaxpr/scatter-add | solution.py:34
  443.8 2.4 copy.35
  448.1 6.7 %scatter_fusion = f32[128,32,128]{2,0,1:T(8,128)S(1)} fusion(f32[128,32,128]{2,0,1:T(8,128)S(1)} %copy.34, s32[48]{0:T(128)S(1)} %fusion.16, f32[48,128,128]{2,1,0:T(8,128)} %bitcast.61), kind=kCustom, calls=%fused_computation.clone.1 | custom fusion | flops 786432 | bytes 9437376 | tf_op jit(solution)/shard_map/while/body/eval_jaxpr/scatter-add | solution.py:34
  465.3 6.7 %scatter_fusion = f32[128,32,128]{2,0,1:T(8,128)S(1)} fusion(f32[128,32,128]{2,0,1:T(8,128)S(1)} %copy.34, s32[48]{0:T(128)S(1)} %fusion.16, f32[48,128,128]{2,1,0:T(8,128)} %bitcast.61), kind=kCustom, calls=%fused_computation.clone.1 | custom fusion | flops 786432 | bytes 9437376 | tf_op jit(solution)/shard_map/while/body/eval_jaxpr/scatter-add | solution.py:34
  482.5 6.7 %scatter_fusion = f32[128,32,128]{2,0,1:T(8,128)S(1)} fusion(f32[128,32,128]{2,0,1:T(8,128)S(1)} %copy.34, s32[48]{0:T(128)S(1)} %fusion.16, f32[48,128,128]{2,1,0:T(8,128)} %bitcast.61), kind=kCustom, calls=%fused_computation.clone.1 | custom fusion | flops 786432 | bytes 9437376 | tf_op jit(solution)/shard_map/while/body/eval_jaxpr/scatter-add | solution.py:34
  499.6 6.7 %scatter_fusion = f32[128,32,128]{2,0,1:T(8,128)S(1)} fusion(f32[128,32,128]{2,0,1:T(8,128)S(1)} %copy.34, s32[48]{0:T(128)S(1)} %fusion.16, f32[48,128,128]{2,1,0:T(8,128)} %bitcast.61), kind=kCustom, calls=%fused_computation.clone.1 | custom fusion | flops 786432 | bytes 9437376 | tf_op jit(solution)/shard_map/while/body/eval_jaxpr/scatter-add | solution.py:34
  516.8 6.7 %scatter_fusion = f32[128,32,128]{2,0,1:T(8,128)S(1)} fusion(f32[128,32,128]{2,0,1:T(8,128)S(1)} %copy.34, s32[48]{0:T(128)S(1)} %fusion.16, f32[48,128,128]{2,1,0:T(8,128)} %bitcast.61), kind=kCustom, calls=%fused_computation.clone.1 | custom fusion | flops 786432 | bytes 9437376 | tf_op jit(solution)/shard_map/while/body/eval_jaxpr/scatter-add | solution.py:34
  534.0 6.7 %scatter_fusion = f32[128,32,128]{2,0,1:T(8,128)S(1)} fusion(f32[128,32,128]{2,0,1:T(8,128)S(1)} %copy.34, s32[48]{0:T(128)S(1)} %fusion.16, f32[48,128,128]{2,1,0:T(8,128)} %bitcast.61), kind=kCustom, calls=%fused_computation.clone.1 | custom fusion | flops 786432 | bytes 9437376 | tf_op jit(solution)/shard_map/while/body/eval_jaxpr/scatter-add | solution.py:34
  542.6 2.9 copy.26
  545.5 52.1 %reduce-scatter.2.cloned.1.call-done = f32[128,512]{1,0:T(8,128)} async-done(((f32[128,4096]{1,0:T(8,128)}), f32[128,512]{1,0:T(8,128)}) %reduce-scatter.2.cloned.1.call-update) | async-done | bytes 262160 | tf_op jit(solution)/shard_map/reduce_scatter | solution.py:54
  (119 shorter events, 144.3 us)
Async XLA Ops:
  6.5 259.7 %all-gather.3.cloned.1.call-start = ((), (), s32[]{:S(2)}) async-start(), calls=%async_computation.2 | async-start | bytes 25952256 | tf_op jit(solution)/shard_map/all_gather | solution.py:51
  21.0 12.8 %copy-start = (s32[4,6]{1,0:T(4,128)S(1)}, s32[4,6]{1,0:T(4,128)}, u32[]{:S(2)}) copy-start(s32[4,6]{1,0:T(4,128)} %param.9) | copy-start | bytes 292
  21.0 167.6 %all-to-all-start = ((bf16[32,128,512]{1,2,0:T(8,128)(2,1)}), bf16[32,128,512]{1,2,0:T(8,128)(2,1)}, u32[]{:S(2)}, u32[]{:S(2)}) async-start(bf16[32,128,512]{1,2,0:T(8,128)(2,1)} %bitcast.65), calls=%async_computation | async-start | bytes 8388608 | tf_op jit(solution)/shard_map/all_to_all | solution.py:46
  33.8 563.8 %reduce-scatter.2.cloned.1.call-start = ((), (), s32[]{:S(2)}) async-start(), calls=%async_computation.3 | async-start | bytes 2359296 | tf_op jit(solution)/shard_map/reduce_scatter | solution.py:54
Sparse Core Ops, SparseCore 0:
  10.1 256.0 all-gather.2
  545.6 51.9 reduce-scatter.1
where the time goes:
time: 608 us; the launch traced here: 604 us
  blocking collectives  155 us (25%)
  local copies, waits for them, and re-layouts  141 us (23%)
  waiting for transfers between devices  130 us (21%)
  other arithmetic  109 us (18%)
  matrix products  33 us (5%)
  between operations  13.4 us (2%)
  starting transfers between devices  12.8 us (2%)
  loops' own time  10.5 us (2%)
    all_gather x1, blocking collectives, body(): lax.all_gather(q_cols, 'row', axis=0, tiled=True)  155 us
    scatter-add x16, other arithmetic, one_group(): tiled.at[:, coarse_ids, :]  108 us
    all_gather x1, waiting for transfers between devices, body(): lax.all_gather(q_tiles, 'row', axis=0, tiled=True)  77.6 us
    reduce_scatter x1, waiting for transfers between devices, body(): return lax.psum_scatter(partial_sum, 'col', scatter_dimension=1, tiled=True)  52.1 us
    reshape x16, local copies, waits for them, and re-layouts, one_group(): product.reshape(height, bundle * per_block, extent)  37.8 us
    dot_general x16, matrix products, one_group(): jnp.einsum('rfa,fkab->rfkb', stripe, bundle_tiles, preferred_element_type...  33 us
    reshape x16, local copies, waits for them, and re-layouts, one_group(): tiled = running.reshape(height, -1, extent)  30.7 us
    scatter-add x16, local copies, waits for them, and re-layouts, one_group(): tiled.at[:, coarse_ids, :]  29.2 us
  transfers between devices with their start and end apart: 3, of which 2 were waited for; matrix products, arithmetic and copies ran while one was open for 2% of the time, Pallas kernels for 0%

commit v1 on v0

--- a/solution.py
+++ b/solution.py
@@ -43,7 +43,10 @@
     extent = p_tiles.shape[2]
     tile_count = lax.axis_size("row")
     expanded = spread_tiles(p_tiles, p_cols, tile_count)
-    transposed = lax.all_to_all(expanded, "row", split_axis=0, concat_axis=1, tiled=True)
+    transposed = jnp.concatenate(
+        lax.all_to_all(jnp.stack(jnp.split(expanded, lax.axis_size("row"), axis=0)), "row", 0, 0),
+        axis=1,
+    )
     empty = jnp.zeros((transposed.shape[0], tile_count * extent), jnp.float32)
     partial_sum = fold_tiles(
         empty,

time: 608 us -> 575 us (0.946)
  waiting for transfers between devices: 130 us -> 75.6 us
  local copies, waits for them, and re-layouts: 141 us -> 173 us
  blocking collectives: 155 us -> 144 us
    all_gather x1, waiting for transfers between devices: 77.6 us -> 22.1 us  [body(): lax.all_gather(q_tiles, 'row', axis=0, tiled=True)]
    unnamed x2 -> x45, local copies, waits for them, and re-layouts: 0.01 us -> 24.2 us
    split x0 -> x34, local copies, waits for them, and re-layouts: none -> 14.1 us  [body(): jnp.split(expanded, lax.axis_size('row'), axis=0)]
    all_gather x1, blocking collectives: 155 us -> 144 us  [body(): lax.all_gather(q_cols, 'row', axis=0, tiled=True)]
    scatter x2 -> x1, local copies, waits for them, and re-layouts: 8.73 us -> 2.27 us  [spread_tiles(): placed = placed.at[columns, :, fine_ids, :].set(flipped)]
  transfers between devices with their start and end apart: 3 -> 3, of which waited for: 2 -> 2; matrix products, arithmetic and copies ran while one was open for 2% -> 8% of each run, Pallas kernels for 0% -> 0%
where the time goes in v1:
time: 575 us; the launch traced here: 571 us
  local copies, waits for them, and re-layouts  173 us (30%)
  blocking collectives  144 us (25%)
  other arithmetic  109 us (19%)
  waiting for transfers between devices  75.6 us (13%)
  matrix products  32.9 us (6%)
  between operations  13.6 us (2%)
  starting transfers between devices  12.8 us (2%)
  loops' own time  10.7 us (2%)
    all_gather x1, blocking collectives, body(): lax.all_gather(q_cols, 'row', axis=0, tiled=True)  144 us
    scatter-add x16, other arithmetic, one_group(): tiled.at[:, coarse_ids, :]  108 us
    reduce_scatter x1, waiting for transfers between devices, body(): return lax.psum_scatter(partial_sum, 'col', scatter_dimension=1, tiled=True)  52.7 us
    reshape x16, local copies, waits for them, and re-layouts, one_group(): product.reshape(height, bundle * per_block, extent)  37.3 us
    dot_general x16, matrix products, one_group(): jnp.einsum('rfa,fkab->rfkb', stripe, bundle_tiles, preferred_element_type...  32.9 us
    reshape x16, local copies, waits for them, and re-layouts, one_group(): tiled = running.reshape(height, -1, extent)  30.7 us
    scatter-add x16, local copies, waits for them, and re-layouts, one_group(): tiled.at[:, coarse_ids, :]  29.5 us
    unnamed x45, local copies, waits for them, and re-layouts  24.2 us
  transfers between devices with their start and end apart: 3, of which 2 were waited for; matrix products, arithmetic and copies ran while one was open for 8% of the time, Pallas kernels for 0%

profile of v1, /device:TPU:1, one launch (start us, length us, event | category | flops | bytes accessed | tf_op | source)
XLA Modules:
  0.0 570.8 jit_solution(5482384697163614812)
XLA Ops:
  9.3 3.0 broadcast_in_dim.18
  53.7 12.8 %all-to-all-start = ((bf16[32,128,512]{1,2,0:T(8,128)(2,1)}), bf16[32,128,512]{1,2,0:T(8,128)(2,1)}, u32[]{:S(2)}, u32[]{:S(2)}) async-start(bf16[32,128,512]{1,2,0:T(8,128)(2,1)} %constant_dynamic-update-slice_fusion), calls=%async_computation | async-start | bytes 8388608 | tf_op jit(solution)/shard_map/all_to_all | solution.py:47
  66.5 143.8 %all-gather = s32[32,4,6]{2,1,0:T(4,128)S(1)} all-gather(s32[1,4,6]{2,1,0:T(4,128)S(1)} %bitcast.130), channel_id=1, replica_groups=mesh['row'=32,'col'=8] {'row'}, dimensions={0}, use_global_device_ids=true | all-gather | bytes 3168 | tf_op jit(solution)/shard_map/all_gather | solution.py:55
  210.4 22.1 %all-gather.3.cloned.1.call-done = bf16[128,6,128,128]{3,2,1,0:T(8,128)(2,1)} async-done(((bf16[4,6,128,128]{3,2,1,0:T(8,128)(2,1)}), bf16[128,6,128,128]{3,2,1,0:T(8,128)(2,1)}) %all-gather.3.cloned.1.call-update) | async-done | bytes 25165840 | tf_op jit(solution)/shard_map/all_gather | solution.py:54
  234.0 274.3 %while.12 = (s32[]{:T(128)}, f32[128,4096]{0,1:T(8,128)}, s32[16,48]{1,0:T(8,128)S(1)}, bf16[16,8,6,128,128]{4,3,2,1,0:T(8,128)(2,1)}, s32[16]{0:T(128)S(1)}, /*...) while((s32[]{:T(128)}, f32[128,4096]{0,1:T(8,128)}, ...), condition=%wide.region_3.4_spmd, body=%wide.region_1.3_spmd.sunk | while | flops 202113168 | bytes 29623528 | solution.py:38
  238.3 2.3 copy.97
  242.6 6.7 %scatter_fusion = f32[128,32,128]{2,0,1:T(8,128)S(1)} fusion(f32[128,32,128]{2,0,1:T(8,128)S(1)} %copy.96, s32[48]{0:T(128)S(1)} %fusion.18, f32[48,128,128]{2,1,0:T(8,128)} %bitcast.92), kind=kCustom, calls=%fused_computation.clone.1 | custom fusion | flops 786432 | bytes 9437376 | tf_op jit(solution)/shard_map/while/body/eval_jaxpr/scatter-add | solution.py:34
  255.5 2.3 copy.97
  259.7 6.7 %scatter_fusion = f32[128,32,128]{2,0,1:T(8,128)S(1)} fusion(f32[128,32,128]{2,0,1:T(8,128)S(1)} %copy.96, s32[48]{0:T(128)S(1)} %fusion.18, f32[48,128,128]{2,1,0:T(8,128)} %bitcast.92), kind=kCustom, calls=%fused_computation.clone.1 | custom fusion | flops 786432 | bytes 9437376 | tf_op jit(solution)/shard_map/while/body/eval_jaxpr/scatter-add | solution.py:34
  272.6 2.3 copy.97
  276.9 6.7 %scatter_fusion = f32[128,32,128]{2,0,1:T(8,128)S(1)} fusion(f32[128,32,128]{2,0,1:T(8,128)S(1)} %copy.96, s32[48]{0:T(128)S(1)} %fusion.18, f32[48,128,128]{2,1,0:T(8,128)} %bitcast.92), kind=kCustom, calls=%fused_computation.clone.1 | custom fusion | flops 786432 | bytes 9437376 | tf_op jit(solution)/shard_map/while/body/eval_jaxpr/scatter-add | solution.py:34
  289.7 2.3 copy.97
  294.0 6.7 %scatter_fusion = f32[128,32,128]{2,0,1:T(8,128)S(1)} fusion(f32[128,32,128]{2,0,1:T(8,128)S(1)} %copy.96, s32[48]{0:T(128)S(1)} %fusion.18, f32[48,128,128]{2,1,0:T(8,128)} %bitcast.92), kind=kCustom, calls=%fused_computation.clone.1 | custom fusion | flops 786432 | bytes 9437376 | tf_op jit(solution)/shard_map/while/body/eval_jaxpr/scatter-add | solution.py:34
  306.9 2.3 copy.97
  311.1 6.7 %scatter_fusion = f32[128,32,128]{2,0,1:T(8,128)S(1)} fusion(f32[128,32,128]{2,0,1:T(8,128)S(1)} %copy.96, s32[48]{0:T(128)S(1)} %fusion.18, f32[48,128,128]{2,1,0:T(8,128)} %bitcast.92), kind=kCustom, calls=%fused_computation.clone.1 | custom fusion | flops 786432 | bytes 9437376 | tf_op jit(solution)/shard_map/while/body/eval_jaxpr/scatter-add | solution.py:34
  324.0 2.3 copy.97
  328.3 6.7 %scatter_fusion = f32[128,32,128]{2,0,1:T(8,128)S(1)} fusion(f32[128,32,128]{2,0,1:T(8,128)S(1)} %copy.96, s32[48]{0:T(128)S(1)} %fusion.18, f32[48,128,128]{2,1,0:T(8,128)} %bitcast.92), kind=kCustom, calls=%fused_computation.clone.1 | custom fusion | flops 786432 | bytes 9437376 | tf_op jit(solution)/shard_map/while/body/eval_jaxpr/scatter-add | solution.py:34
  341.2 2.3 copy.97
  345.4 6.7 %scatter_fusion = f32[128,32,128]{2,0,1:T(8,128)S(1)} fusion(f32[128,32,128]{2,0,1:T(8,128)S(1)} %copy.96, s32[48]{0:T(128)S(1)} %fusion.18, f32[48,128,128]{2,1,0:T(8,128)} %bitcast.92), kind=kCustom, calls=%fused_computation.clone.1 | custom fusion | flops 786432 | bytes 9437376 | tf_op jit(solution)/shard_map/while/body/eval_jaxpr/scatter-add | solution.py:34
  358.3 2.3 copy.97
  362.6 6.7 %scatter_fusion = f32[128,32,128]{2,0,1:T(8,128)S(1)} fusion(f32[128,32,128]{2,0,1:T(8,128)S(1)} %copy.96, s32[48]{0:T(128)S(1)} %fusion.18, f32[48,128,128]{2,1,0:T(8,128)} %bitcast.92), kind=kCustom, calls=%fused_computation.clone.1 | custom fusion | flops 786432 | bytes 9437376 | tf_op jit(solution)/shard_map/while/body/eval_jaxpr/scatter-add | solution.py:34
  375.5 2.3 copy.97
  379.7 6.7 %scatter_fusion = f32[128,32,128]{2,0,1:T(8,128)S(1)} fusion(f32[128,32,128]{2,0,1:T(8,128)S(1)} %copy.96, s32[48]{0:T(128)S(1)} %fusion.18, f32[48,128,128]{2,1,0:T(8,128)} %bitcast.92), kind=kCustom, calls=%fused_computation.clone.1 | custom fusion | flops 786432 | bytes 9437376 | tf_op jit(solution)/shard_map/while/body/eval_jaxpr/scatter-add | solution.py:34
  396.9 6.7 %scatter_fusion = f32[128,32,128]{2,0,1:T(8,128)S(1)} fusion(f32[128,32,128]{2,0,1:T(8,128)S(1)} %copy.96, s32[48]{0:T(128)S(1)} %fusion.18, f32[48,128,128]{2,1,0:T(8,128)} %bitcast.92), kind=kCustom, calls=%fused_computation.clone.1 | custom fusion | flops 786432 | bytes 9437376 | tf_op jit(solution)/shard_map/while/body/eval_jaxpr/scatter-add | solution.py:34
  414.0 6.7 %scatter_fusion = f32[128,32,128]{2,0,1:T(8,128)S(1)} fusion(f32[128,32,128]{2,0,1:T(8,128)S(1)} %copy.96, s32[48]{0:T(128)S(1)} %fusion.18, f32[48,128,128]{2,1,0:T(8,128)} %bitcast.92), kind=kCustom, calls=%fused_computation.clone.1 | custom fusion | flops 786432 | bytes 9437376 | tf_op jit(solution)/shard_map/while/body/eval_jaxpr/scatter-add | solution.py:34
  431.1 6.7 %scatter_fusion = f32[128,32,128]{2,0,1:T(8,128)S(1)} fusion(f32[128,32,128]{2,0,1:T(8,128)S(1)} %copy.96, s32[48]{0:T(128)S(1)} %fusion.18, f32[48,128,128]{2,1,0:T(8,128)} %bitcast.92), kind=kCustom, calls=%fused_computation.clone.1 | custom fusion | flops 786432 | bytes 9437376 | tf_op jit(solution)/shard_map/while/body/eval_jaxpr/scatter-add | solution.py:34
  448.3 6.7 %scatter_fusion = f32[128,32,128]{2,0,1:T(8,128)S(1)} fusion(f32[128,32,128]{2,0,1:T(8,128)S(1)} %copy.96, s32[48]{0:T(128)S(1)} %fusion.18, f32[48,128,128]{2,1,0:T(8,128)} %bitcast.92), kind=kCustom, calls=%fused_computation.clone.1 | custom fusion | flops 786432 | bytes 9437376 | tf_op jit(solution)/shard_map/while/body/eval_jaxpr/scatter-add | solution.py:34
  465.4 6.7 %scatter_fusion = f32[128,32,128]{2,0,1:T(8,128)S(1)} fusion(f32[128,32,128]{2,0,1:T(8,128)S(1)} %copy.96, s32[48]{0:T(128)S(1)} %fusion.18, f32[48,128,128]{2,1,0:T(8,128)} %bitcast.92), kind=kCustom, calls=%fused_computation.clone.1 | custom fusion | flops 786432 | bytes 9437376 | tf_op jit(solution)/shard_map/while/body/eval_jaxpr/scatter-add | solution.py:34
  482.6 6.7 %scatter_fusion = f32[128,32,128]{2,0,1:T(8,128)S(1)} fusion(f32[128,32,128]{2,0,1:T(8,128)S(1)} %copy.96, s32[48]{0:T(128)S(1)} %fusion.18, f32[48,128,128]{2,1,0:T(8,128)} %bitcast.92), kind=kCustom, calls=%fused_computation.clone.1 | custom fusion | flops 786432 | bytes 9437376 | tf_op jit(solution)/shard_map/while/body/eval_jaxpr/scatter-add | solution.py:34
  499.7 6.7 %scatter_fusion = f32[128,32,128]{2,0,1:T(8,128)S(1)} fusion(f32[128,32,128]{2,0,1:T(8,128)S(1)} %copy.96, s32[48]{0:T(128)S(1)} %fusion.18, f32[48,128,128]{2,1,0:T(8,128)} %bitcast.92), kind=kCustom, calls=%fused_computation.clone.1 | custom fusion | flops 786432 | bytes 9437376 | tf_op jit(solution)/shard_map/while/body/eval_jaxpr/scatter-add | solution.py:34
  508.3 2.9 copy.88
  511.2 52.7 %reduce-scatter.2.cloned.1.call-done = f32[128,512]{1,0:T(8,128)} async-done(((f32[128,4096]{1,0:T(8,128)}), f32[128,512]{1,0:T(8,128)}) %reduce-scatter.2.cloned.1.call-update) | async-done | bytes 262160 | tf_op jit(solution)/shard_map/reduce_scatter | solution.py:57
  (196 shorter events, 180.4 us)
Async XLA Ops:
  6.5 226.0 %all-gather.3.cloned.1.call-start = ((), (), s32[]{:S(2)}) async-start(), calls=%async_computation.2 | async-start | bytes 25952256 | tf_op jit(solution)/shard_map/all_gather | solution.py:54
  23.7 8.7 %copy-start = (bf16[1,128,4,128]{1,3,2,0:T(8,128)(2,1)S(1)}, bf16[1,128,4,128]{1,3,2,0:T(8,128)(2,1)}, u32[]{:S(2)}) copy-start(bf16[1,128,4,128]{1,3,2,0:T(8,128)(2,1)} %copy.59) | copy-start | bytes 393220
  24.5 7.2 %copy-start.1 = (bf16[1,128,4,128]{1,3,2,0:T(8,128)(2,1)S(1)}, bf16[1,128,4,128]{1,3,2,0:T(8,128)(2,1)}, u32[]{:S(2)}) copy-start(bf16[1,128,4,128]{1,3,2,0:T(8,128)(2,1)} %copy.58) | copy-start | bytes 393220
  25.3 5.8 %copy-start.2 = (bf16[1,128,4,128]{1,3,2,0:T(8,128)(2,1)S(1)}, bf16[1,128,4,128]{1,3,2,0:T(8,128)(2,1)}, u32[]{:S(2)}) copy-start(bf16[1,128,4,128]{1,3,2,0:T(8,128)(2,1)} %copy.57) | copy-start | bytes 393220
  26.1 4.4 copy-start.3
  28.8 14.3 %copy-start.5 = (bf16[1,128,4,128]{1,3,2,0:T(8,128)(2,1)S(1)}, bf16[1,128,4,128]{1,3,2,0:T(8,128)(2,1)}, u32[]{:S(2)}) copy-start(bf16[1,128,4,128]{1,3,2,0:T(8,128)(2,1)} %copy.71) | copy-start | bytes 393220
  28.8 15.0 %copy-start.4 = (bf16[1,128,4,128]{1,3,2,0:T(8,128)(2,1)S(1)}, bf16[1,128,4,128]{1,3,2,0:T(8,128)(2,1)}, u32[]{:S(2)}) copy-start(bf16[1,128,4,128]{1,3,2,0:T(8,128)(2,1)} %copy.72) | copy-start | bytes 393220
  53.7 12.8 %copy-start.6 = (s32[4,6]{1,0:T(4,128)S(1)}, s32[4,6]{1,0:T(4,128)}, u32[]{:S(2)}) copy-start(s32[4,6]{1,0:T(4,128)} %param.9) | copy-start | bytes 292
  53.7 156.7 %all-to-all-start = ((bf16[32,128,512]{1,2,0:T(8,128)(2,1)}), bf16[32,128,512]{1,2,0:T(8,128)(2,1)}, u32[]{:S(2)}, u32[]{:S(2)}) async-start(bf16[32,128,512]{1,2,0:T(8,128)(2,1)} %constant_dynamic-update-slice_fusion), calls=%async_computation | async-start | bytes 8388608 | tf_op jit(solution)/shard_map/all_to_all | solution.py:47
  66.5 497.5 %reduce-scatter.2.cloned.1.call-start = ((), (), s32[]{:S(2)}) async-start(), calls=%async_computation.3 | async-start | bytes 2359296 | tf_op jit(solution)/shard_map/reduce_scatter | solution.py:57
Sparse Core Ops, SparseCore 0:
  10.1 222.3 all-gather.2
  511.3 52.5 reduce-scatter.1
